TPU v7x, 32 devices: a whole 2x2x4 slice. The times are simulated.
32 devices in a mesh: row: 8 (over z, y), col: 4 (over x, core).
Axes of the slice: x: 2, y: 2, z: 4, core: 2. Of those that a mesh axis runs over, the one named last changes fastest.
Arguments:
- anc_inverse: float32 [20480, 20480], P('row', 'col'), may hold values from -6 to 6
- l_store: float32 [4, 20480, 256], P('col', 'row'), may hold values from -0.0546875 to 0.0546875
- diag_inv: float32 [4, 256, 256], P('col'), may hold values from -6 to 6
- block_lists: int32 [4, 96], replicated, may hold values from 0 to 159, as said below
- block_counts: int32 [4], replicated, may hold values from 48 to 96, as said below
- sibling_columns: int32 [4], replicated, may hold values from 0 to 3, as said below
Outputs:
- upper_out: float32 [4, 256, 20480], P(None, 'row', 'col')
- lower_out: float32 [4, 20480, 256], P('col', 'row')
- diag_out: float32 [4, 256, 256], P('col')
Inputs may be any that keep to these rules, and one draw needn't show every extreme that they name: `block_lists`: in each sibling's row the entries are distinct block indices; entries at positions from block_counts onward are ignored. `block_counts`: some sibling uses all 96 entries. `sibling_columns`: distinct columns for distinct siblings.
All inputs are finite; a program needn't handle non-finite values.
Results may differ from a plain program's by a relative error of at most 0.00011.
Values sent between devices are 32-bit elements; how exact they have to be, the bound alone decides.
A program may use at most 128 MiB of HBM per device.

v0:
```python
import jax
import jax.numpy as jnp
from jax import lax
from jax.sharding import PartitionSpec as P

BLK = 128


def broadcast(block, axis, source):
    block = jnp.where(lax.axis_index(axis) == source, block, jnp.zeros_like(block))
    return lax.psum(block, axis)


def listed_blocks(block_lists, block_counts, first_block, block_total):
    block_ids = first_block + jnp.arange(block_total, dtype=jnp.int32)
    valid_entry = jnp.arange(block_lists.shape[1], dtype=jnp.int32)[None, :] < block_counts[:, None]
    entry_hits = (block_lists[:, :, None] == block_ids[None, None, :]) & valid_entry[:, :, None]
    return jnp.repeat(jnp.any(entry_hits, axis=1).astype(jnp.float32), BLK, axis=1)


def per_device(anc_inverse, l_store, diag_inv, block_lists, block_counts, sibling_columns):
    row_cells = anc_inverse.shape[0]
    col_cells = anc_inverse.shape[1]
    siblings = block_lists.shape[0]
    col_count = lax.axis_size("col")
    row_index = lax.axis_index("row")
    col_index = lax.axis_index("col")
    row_mask = listed_blocks(
        block_lists, block_counts, row_index * (row_cells // BLK), row_cells // BLK
    )
    col_mask = listed_blocks(
        block_lists, block_counts, col_index * (col_cells // BLK), col_cells // BLK
    )
    own_slot = l_store[0]
    chosen = (sibling_columns == col_index).astype(jnp.float32)
    stacked = jnp.stack(
        [broadcast(own_slot, "col", sibling_columns[sibling]) for sibling in range(siblings)]
    )
    masked = stacked * row_mask[:, :, None]
    partial_value = (
        -jnp.einsum(
            "jrw,rc->jwc",
            masked,
            anc_inverse,
            precision=lax.Precision.HIGHEST,
            preferred_element_type=jnp.float32,
        )
        * col_mask[:, None, :]
    )
    upper_part = lax.psum_scatter(partial_value, "row", scatter_dimension=1, tiled=True)
    owner_table = (
        sibling_columns[:, None] == jnp.arange(col_count, dtype=jnp.int32)[None, :]
    ).astype(jnp.float32)
    slots = jnp.einsum(
        "jc,jwt->wct",
        owner_table,
        upper_part,
        precision=lax.Precision.HIGHEST,
        preferred_element_type=jnp.float32,
    )
    slots = slots.reshape(slots.shape[0], col_count * col_cells)
    by_owner = lax.all_to_all(slots, "col", split_axis=1, concat_axis=1, tiled=True)
    picked = lax.all_to_all(by_owner, "row", split_axis=1, concat_axis=0, tiled=True)
    own_panel = jnp.sum(chosen[:, None, None] * masked, axis=0)
    inner_sum = jnp.dot(
        picked, own_panel, precision=lax.Precision.HIGHEST, preferred_element_type=jnp.float32
    )
    diag_total = lax.psum(inner_sum, "row")
    present = jnp.sum(chosen)
    diag_out = (present * diag_inv[0] - diag_total)[None]
    lower_out = jnp.transpose(picked)[None]
    return (upper_part, lower_out, diag_out)


def solution(mesh):
    return jax.shard_map(
        per_device,
        mesh=mesh,
        in_specs=(P("row", "col"), P("col", "row", None), P("col", None, None), P(), P(), P()),
        out_specs=(P(None, "row", "col"), P("col", "row", None), P("col", None, None)),
        check_vma=False,
    )
```

profile of v0, /device:TPU:0, one launch (start us, length us, event | category | flops | bytes accessed | tf_op | source)
XLA Modules:
  0.0 934.0 jit_solution(856084657477815547)
XLA Ops:
  7.2 0.0 all-reduce.6.cloned.1.call-start
  7.2 1.5 fusion.12
  11.3 6.0 broadcast_select_fusion.3
  17.3 0.0 copy-start.3
  17.3 0.0 copy-start.2
  17.3 0.0 all-reduce.6.cloned.1.call-update
  17.3 0.0 reduce-scatter.2.cloned.1.call-start
  17.4 0.6 copy-done.3
  17.9 0.1 iota_compare_fusion.1
  18.0 0.0 copy-done.2
  18.0 0.2 and_reduce_fusion
  18.2 0.1 broadcast_bitcast_fusion
  18.4 0.5 and_reduce_fusion.1
  18.9 0.1 copy.39
  19.0 0.1 broadcast_bitcast_fusion.1
  19.1 187.9 %all-reduce.6.cloned.1.call-done = (f32[1,2560,256]{2,1,0:T(8,128)}, f32[1,2560,256]{2,1,0:T(8,128)}, f32[1,2560,256]{2,1,0:T(8,128)}, f32[1,2560,256]{2,1,0:T(8,128)}) async-done(((f32[1,2560,256]{2,1,0:T(8,128)}, f32[1,2560,256]{2,1,0:T(8,128)}, f32[1,2560,256]{2,1,0:T(8,128)}, f32[1,2560,256]{2,1,0:T(8,128)}), (f32[1,2560,256]{2,1,0:T(8,128)}, f32[1,2560,256]{2,1,0:T(8,128)}, f32[1,2560,256]{2,1,0:T(8,128)}, ...) | async-done | bytes 10485776 | tf_op jit(solution)/shard_map/psum | solution.py:11
  207.0 188.3 %negate_multiply_fusion = f32[4,256,5120]{2,1,0:T(8,128)} fusion(f32[2560,5120]{1,0:T(8,128)} %param.6, f32[4,5120]{1,0:T(4,128)S(1)} %bitcast.44, f32[1,2560,256]{2,1,0:T(8,128)} %get-tuple-element.21, f32[1,2560,256]{2,1,0:T(8,128)} %get-tuple-element.22, f32[1,2560,256]{2,1,0:T(8,128)} %get-tuple-element.23, f32[1,2560,256]{2,1,0:T(8,128)} %get-tuple-element.24, ...), kind=kOutput, calls=%fused_computation.2 | convolution fusion | flops 161082245120 | bytes 84008960 | tf_op jit(solution)/shard_map/jrw,rc->jwc/dot_general | solution.py:41
  395.2 0.0 copy-start.1
  395.2 0.0 reduce-scatter.2.cloned.1.call-update
  395.3 342.8 %reduce-scatter.2.cloned.1.call-done = f32[4,32,5120]{2,1,0:T(8,128)} async-done(((f32[4,256,5120]{2,1,0:T(8,128)}), f32[4,32,5120]{2,1,0:T(8,128)}) %reduce-scatter.2.cloned.1.call-update) | async-done | bytes 2621456 | tf_op jit(solution)/shard_map/reduce_scatter | solution.py:50
  738.1 0.0 copy-done.1
  738.1 5.8 convolution_bitcast_fusion
  743.9 1.5 copy.42
  745.4 33.8 %all_to_all.25 = f32[32,4,5120]{2,0,1:T(8,128)S(1)} all-to-all(f32[32,4,5120]{2,0,1:T(8,128)S(1)} %copy.42), channel_id=1, replica_groups=mesh['row'=8,'col'=4] {'col'}, dimensions={1} | all-to-all | bytes 5242880 | tf_op jit(solution)/shard_map/all_to_all | solution.py:62
  779.2 1.7 copy.43
  780.9 2.1 all_to_all.19
  783.1 4.8 copy.44
  787.8 3.7 all-to-all-start.1
  791.6 0.0 all-reduce.4.cloned.1.call-start
  791.6 0.6 fusion.11
  792.2 7.0 multiply_reduce_fusion
  799.3 51.5 %all-to-all-done.1 = f32[32,8,2560]{2,0,1:T(8,128)S(1)} async-done(((f32[32,8,2560]{2,0,1:T(8,128)}), f32[32,8,2560]{2,0,1:T(8,128)S(1)}, u32[]{:S(2)}, u32[]{:S(2)}) %all-to-all-start.1) | async-done | bytes 2621472 | tf_op jit(solution)/shard_map/all_to_all | solution.py:63
  850.8 4.8 fusion.13
  855.5 0.0 all-reduce.4.cloned.1.call-update
  855.5 0.0 copy-start
  855.6 2.1 copy.45
  857.6 67.5 %all-reduce.4.cloned.1.call-done = f32[256,256]{1,0:T(8,128)} async-done(((f32[256,256]{1,0:T(8,128)}), f32[256,256]{1,0:T(8,128)}) %all-reduce.4.cloned.1.call-update) | async-done | bytes 262160 | tf_op jit(solution)/shard_map/psum | solution.py:68
  925.1 0.0 copy-done
  925.1 2.3 fusion.6
  (6 shorter events, 0.1 us)
Async XLA Ops:
  7.2 199.8 %all-reduce.6.cloned.1.call-start = ((), (), s32[]{:S(2)}) async-start(), calls=%async_computation.5 | async-start | bytes 20971520 | tf_op jit(solution)/shard_map/psum | solution.py:11
  17.3 0.7 copy-start.3
  17.3 0.7 copy-start.2
  17.3 720.8 %reduce-scatter.2.cloned.1.call-start = ((), (), s32[]{:S(2)}) async-start(), calls=%async_computation.3 | async-start | bytes 23592960 | tf_op jit(solution)/shard_map/reduce_scatter | solution.py:50
  395.2 342.9 %copy-start.1 = (s32[4]{0:T(128)S(1)}, s32[4]{0:T(128)}, u32[]{:S(2)}) copy-start(s32[4]{0:T(128)} %param.11) | copy-start | bytes 52
  787.8 62.9 %all-to-all-start.1 = ((f32[32,8,2560]{2,0,1:T(8,128)}), f32[32,8,2560]{2,0,1:T(8,128)S(1)}, u32[]{:S(2)}, u32[]{:S(2)}) async-start(f32[32,8,2560]{2,0,1:T(8,128)} %copy.44), calls=%async_computation.2 | async-start | bytes 5242880 | tf_op jit(solution)/shard_map/all_to_all | solution.py:63
  791.6 133.6 %all-reduce.4.cloned.1.call-start = ((), (), s32[]{:S(2)}) async-start(), calls=%async_computation.4 | async-start | bytes 524288 | tf_op jit(solution)/shard_map/psum | solution.py:68
  855.5 69.6 %copy-start = (f32[1,256,256]{2,1,0:T(8,128)S(1)}, f32[1,256,256]{2,1,0:T(8,128)}, u32[]{:S(2)}) copy-start(f32[1,256,256]{2,1,0:T(8,128)} %param.8) | copy-start | bytes 786436
Sparse Core Ops, SparseCore 0:
  17.4 189.5 all-reduce.5
  395.4 342.6 reduce-scatter.1
  855.7 69.4 all-reduce.3
where the time goes:
time: 934 us
  waiting for transfers between devices  650 us (70%)
  matrix products  199 us (21%)
  blocking collectives  33.8 us (4%)
  other arithmetic  16.7 us (2%)
  between operations  16.5 us (2%)
  local copies, waits for them, and re-layouts  14.6 us (2%)
    reduce_scatter x1, waiting for transfers between devices, per_device(): lax.psum_scatter(partial_value, 'row', scatter_dimension=1, tiled=True)  343 us
    dot_general x1, matrix products, per_device(): jnp.einsum('jrw,rc->jwc', masked, anc_inverse, precision=lax.Precision.HI...  188 us
    psum x1, waiting for transfers between devices, broadcast(): return lax.psum(block, axis)  188 us
    psum x1, waiting for transfers between devices, per_device(): diag_total = lax.psum(inner_sum, 'row')  67.5 us
    all_to_all x1, waiting for transfers between devices, per_device(): lax.all_to_all(by_owner, 'row', split_axis=1, concat_axis=0, tiled=True)  51.5 us
    all_to_all x1, blocking collectives, per_device(): lax.all_to_all(slots, 'col', split_axis=1, concat_axis=1, tiled=True)  33.8 us
  transfers between devices with their start and end apart: 4, of which 4 were waited for; matrix products, arithmetic and copies ran while one was open for 1% of the time, Pallas kernels for 0%

commit v1 on v0

--- a/solution.py
+++ b/solution.py
@@ -65,7 +65,11 @@
     inner_sum = jnp.dot(
         picked, own_panel, precision=lax.Precision.HIGHEST, preferred_element_type=jnp.float32
     )
-    diag_total = lax.psum(inner_sum, "row")
+    diag_total = inner_sum
+    for hop in (1, 2, 4):
+        diag_total = diag_total + lax.ppermute(
+            diag_total, "row", [(dev, dev ^ hop) for dev in range(8)]
+        )
     present = jnp.sum(chosen)
     diag_out = (present * diag_inv[0] - diag_total)[None]
     lower_out = jnp.transpose(picked)[None]

time: 934 us -> 891 us (0.954)
  waiting for transfers between devices: 650 us -> 602 us
    psum x1 -> x0, waiting for transfers between devices: 67.5 us -> none  [per_device(): diag_total = lax.psum(inner_sum, 'row')]
    ppermute x0 -> x3, waiting for transfers between devices: none -> 19.8 us  [per_device(): lax.ppermute(diag_total, 'row', [(dev, dev ^ hop) for dev in range(8)])]
  transfers between devices with their start and end apart: 4 -> 6, of which waited for: 4 -> 6; matrix products, arithmetic and copies ran while one was open for 1% -> 1% of each run, Pallas kernels for 0% -> 0%
where the time goes in v1:
time: 891 us
  waiting for transfers between devices  602 us (68%)
  matrix products  198 us (22%)
  blocking collectives  33.8 us (4%)
  between operations  16.7 us (2%)
  other arithmetic  15.7 us (2%)
  local copies, waits for them, and re-layouts  14.5 us (2%)
  starting transfers between devices  9.63 us (1%)
    reduce_scatter x1, waiting for transfers between devices, per_device(): lax.psum_scatter(partial_value, 'row', scatter_dimension=1, tiled=True)  343 us
    dot_general x1, matrix products, per_device(): jnp.einsum('jrw,rc->jwc', masked, anc_inverse, precision=lax.Precision.HI...  188 us
    psum x1, waiting for transfers between devices, broadcast(): return lax.psum(block, axis)  188 us
    all_to_all x1, waiting for transfers between devices, per_device(): lax.all_to_all(by_owner, 'row', split_axis=1, concat_axis=0, tiled=True)  51.6 us
    all_to_all x1, blocking collectives, per_device(): lax.all_to_all(slots, 'col', split_axis=1, concat_axis=1, tiled=True)  33.8 us
    ppermute x3, waiting for transfers between devices, per_device(): lax.ppermute(diag_total, 'row', [(dev, dev ^ hop) for dev in range(8)])  19.8 us
  transfers between devices with their start and end apart: 6, of which 6 were waited for; matrix products, arithmetic and copies ran while one was open for 1% of the time, Pallas kernels for 0%

profile of v1, /device:TPU:0, one launch (start us, length us, event | category | flops | bytes accessed | tf_op | source)
XLA Modules:
  0.0 891.0 jit_solution(14223723122934568616)
XLA Ops:
  7.2 0.0 all-reduce.3.cloned.1.call-start
  7.2 1.5 fusion.12
  11.3 5.9 broadcast_select_fusion.3
  17.2 0.0 copy-start.3
  17.2 0.0 copy-start.2
  17.2 0.0 all-reduce.3.cloned.1.call-update
  17.2 0.0 reduce-scatter.2.cloned.1.call-start
  17.3 0.6 copy-done.3
  17.8 0.1 iota_compare_fusion.1
  17.9 0.0 copy-done.2
  17.9 0.2 and_reduce_fusion
  18.1 0.1 broadcast_bitcast_fusion
  18.3 0.5 and_reduce_fusion.1
  18.8 0.1 copy.39
  18.9 0.1 broadcast_bitcast_fusion.1
  19.0 187.9 %all-reduce.3.cloned.1.call-done = (f32[1,2560,256]{2,1,0:T(8,128)}, f32[1,2560,256]{2,1,0:T(8,128)}, f32[1,2560,256]{2,1,0:T(8,128)}, f32[1,2560,256]{2,1,0:T(8,128)}) async-done(((f32[1,2560,256]{2,1,0:T(8,128)}, f32[1,2560,256]{2,1,0:T(8,128)}, f32[1,2560,256]{2,1,0:T(8,128)}, f32[1,2560,256]{2,1,0:T(8,128)}), (f32[1,2560,256]{2,1,0:T(8,128)}, f32[1,2560,256]{2,1,0:T(8,128)}, f32[1,2560,256]{2,1,0:T(8,128)}, ...) | async-done | bytes 10485776 | tf_op jit(solution)/shard_map/psum | solution.py:11
  206.9 188.3 %negate_multiply_fusion = f32[4,256,5120]{2,1,0:T(8,128)} fusion(f32[2560,5120]{1,0:T(8,128)} %param.6, f32[4,5120]{1,0:T(4,128)S(1)} %bitcast.44, f32[1,2560,256]{2,1,0:T(8,128)} %get-tuple-element.21, f32[1,2560,256]{2,1,0:T(8,128)} %get-tuple-element.22, f32[1,2560,256]{2,1,0:T(8,128)} %get-tuple-element.23, f32[1,2560,256]{2,1,0:T(8,128)} %get-tuple-element.24, ...), kind=kOutput, calls=%fused_computation.2 | convolution fusion | flops 161082245120 | bytes 84008960 | tf_op jit(solution)/shard_map/jrw,rc->jwc/dot_general | solution.py:41
  395.2 0.0 copy-start.1
  395.2 0.0 reduce-scatter.2.cloned.1.call-update
  395.2 343.1 %reduce-scatter.2.cloned.1.call-done = f32[4,32,5120]{2,1,0:T(8,128)} async-done(((f32[4,256,5120]{2,1,0:T(8,128)}), f32[4,32,5120]{2,1,0:T(8,128)}) %reduce-scatter.2.cloned.1.call-update) | async-done | bytes 2621456 | tf_op jit(solution)/shard_map/reduce_scatter | solution.py:50
  738.4 0.0 copy-done.1
  738.4 5.8 convolution_bitcast_fusion
  744.1 1.5 copy.42
  745.7 33.8 %all_to_all.25 = f32[32,4,5120]{2,0,1:T(8,128)S(1)} all-to-all(f32[32,4,5120]{2,0,1:T(8,128)S(1)} %copy.42), channel_id=1, replica_groups=mesh['row'=8,'col'=4] {'col'}, dimensions={1} | all-to-all | bytes 5242880 | tf_op jit(solution)/shard_map/all_to_all | solution.py:62
  779.5 1.7 copy.43
  781.2 2.1 all_to_all.19
  783.3 4.8 copy.44
  788.1 3.8 all-to-all-start.1
  791.9 0.7 fusion.11
  792.6 6.8 multiply_reduce_fusion
  799.4 51.6 %all-to-all-done.1 = f32[32,8,2560]{2,0,1:T(8,128)S(1)} async-done(((f32[32,8,2560]{2,0,1:T(8,128)}), f32[32,8,2560]{2,0,1:T(8,128)S(1)}, u32[]{:S(2)}, u32[]{:S(2)}) %all-to-all-start.1) | async-done | bytes 2621472 | tf_op jit(solution)/shard_map/all_to_all | solution.py:63
  851.0 4.0 fusion.13
  855.1 1.5 collective-permute-start
  856.6 5.6 collective-permute-done
  862.2 0.8 collective-permute-start.1
  863.0 5.6 collective-permute-done.1
  868.7 3.3 collective-permute-start.2
  872.1 0.0 copy-start
  872.1 2.1 copy.45
  874.1 8.6 collective-permute-done.2
  882.7 0.0 copy-done
  882.7 1.4 fusion.6
  (8 shorter events, 0.1 us)
Async XLA Ops:
  7.2 199.7 %all-reduce.3.cloned.1.call-start = ((), (), s32[]{:S(2)}) async-start(), calls=%async_computation.4 | async-start | bytes 20971520 | tf_op jit(solution)/shard_map/psum | solution.py:11
  17.2 0.7 copy-start.3
  17.2 0.7 copy-start.2
  17.2 721.1 %reduce-scatter.2.cloned.1.call-start = ((), (), s32[]{:S(2)}) async-start(), calls=%async_computation.3 | async-start | bytes 23592960 | tf_op jit(solution)/shard_map/reduce_scatter | solution.py:50
  395.2 343.2 %copy-start.1 = (s32[4]{0:T(128)S(1)}, s32[4]{0:T(128)}, u32[]{:S(2)}) copy-start(s32[4]{0:T(128)} %param.11) | copy-start | bytes 52
  788.1 62.9 %all-to-all-start.1 = ((f32[32,8,2560]{2,0,1:T(8,128)}), f32[32,8,2560]{2,0,1:T(8,128)S(1)}, u32[]{:S(2)}, u32[]{:S(2)}) async-start(f32[32,8,2560]{2,0,1:T(8,128)} %copy.44), calls=%async_computation.2 | async-start | bytes 5242880 | tf_op jit(solution)/shard_map/all_to_all | solution.py:63
  855.1 7.1 collective-permute-start
  862.2 6.5 collective-permute-start.1
  868.7 14.0 %collective-permute-start.2 = (f32[256,256]{1,0:T(8,128)S(1)}, f32[256,256]{1,0:T(8,128)S(1)}, u32[]{:S(2)}, u32[]{:S(2)}) collective-permute-start(f32[256,256]{1,0:T(8,128)S(1)} %add.44), channel_id=1, source_target_pairs={{0,16},{4,20},{8,24},{12,28},{16,0},{20,4},{24,8},{28,12},{1,17},{... | collective-permute-start | bytes 786440 | tf_op jit(solution)/shard_map/ppermute | solution.py:70
  872.1 10.7 %copy-start = (f32[1,256,256]{2,1,0:T(8,128)S(1)}, f32[1,256,256]{2,1,0:T(8,128)}, u32[]{:S(2)}) copy-start(f32[1,256,256]{2,1,0:T(8,128)} %param.8) | copy-start | bytes 786436
Sparse Core Ops, SparseCore 0:
  17.3 189.5 all-reduce.2
  395.4 342.9 reduce-scatter.1
